TPU v7x, 32 devices: a whole 2x2x4 slice. The times are simulated.
32 devices in a mesh: chan: 4 (over y, x), space: 8 (over z, core).
Axes of the slice: x: 2, y: 2, z: 4, core: 2. Of those that a mesh axis runs over, the one named last changes fastest.
Arguments:
- volume: bfloat16 [32, 16, 256, 128], P('space', None, 'chan'), may hold values from -6 to 6
- kernel: bfloat16 [27, 256, 256], P(None, 'chan'), may hold values from -0.078125 to 0.078125
- bias: float32 [256], P('chan'), may hold values from -3 to 3
- cotangent: bfloat16 [32, 16, 256, 128], P('space', None, 'chan'), may hold values from -6 to 6
Outputs:
- output: bfloat16 [32, 16, 256, 128], P('space', None, 'chan')
- input_grad: bfloat16 [32, 16, 256, 128], P('space', None, 'chan')
- weight_grad: float32 [27, 256, 256], P(None, 'chan')
All inputs are finite; a program needn't handle non-finite values.
Results may differ from a plain program's by a relative error of at most 0.0049.
Values may be sent and summed in bfloat16 or wider, within the bound.
A program may use at most 128 MiB of HBM per device.

v0:
```python
import math

import jax
import jax.numpy as jnp
from jax import lax
from jax.sharding import PartitionSpec as P


def padded_2(cells, sides, width):
    for axis, dim in sides:
        count = lax.axis_size(axis)
        ends = count - 1
        head = lax.slice_in_dim(cells, 0, width, axis=dim)
        tail = lax.slice_in_dim(cells, cells.shape[dim] - width, cells.shape[dim], axis=dim)
        cells = jnp.concatenate(
            [
                lax.ppermute(tail, axis, [(i, (i + 1) % count) for i in range(ends)]),
                cells,
                lax.ppermute(head, axis, [((i + 1) % count, i) for i in range(ends)]),
            ],
            axis=dim,
        )
    return cells


def tap_list():
    return [
        (first, second, third) for first in range(3) for second in range(3) for third in range(3)
    ]


def pad_sides(field):
    return jnp.pad(field, ((0, 0), (1, 1), (0, 0), (1, 1)))


def on_device(volume, kernel, bias, cotangent):
    size_x, size_y, chans_local, size_z = volume.shape
    out_local = kernel.shape[1]
    whole_chans = lax.all_gather(volume, "chan", axis=2, tiled=True)
    gathered = padded_2(whole_chans, (("space", 0),), 1)
    padded = pad_sides(gathered)
    chans_total = padded.shape[2]
    accum = jnp.zeros((size_x, size_y, out_local, size_z), jnp.float32)
    for index_tap, (first, second, third) in enumerate(tap_list()):
        slab = padded[first : first + size_x, second : second + size_y, :, third : third + size_z]
        accum = accum + jnp.einsum(
            "oc,xycz->xyoz", kernel[index_tap], slab, preferred_element_type=jnp.float32
        )
    pre = accum + bias.reshape(1, 1, out_local, 1)
    sigmoid_pre = jax.nn.sigmoid(pre)
    output = (pre * sigmoid_pre).astype(jnp.bfloat16)
    grad_pre = (
        cotangent.astype(jnp.float32) * sigmoid_pre * (1.0 + pre * (1.0 - sigmoid_pre))
    ).astype(jnp.bfloat16)
    partials = []
    for index_tap, (first, second, third) in enumerate(tap_list()):
        slab = padded[first : first + size_x, second : second + size_y, :, third : third + size_z]
        partials.append(
            jnp.einsum("xyoz,xycz->oc", grad_pre, slab, preferred_element_type=jnp.float32)
        )
    summed = lax.psum(jnp.stack(partials), "space")
    weight_grad = summed / math.sqrt(size_x * size_y * size_z * lax.axis_size("space"))
    grad_rim = padded_2(grad_pre, (("space", 0),), 1)
    grad_padded = pad_sides(grad_rim)
    stacked = jnp.concatenate(
        [
            grad_padded[
                2 - first : 2 - first + size_x,
                2 - second : 2 - second + size_y,
                :,
                2 - third : 2 - third + size_z,
            ]
            for first, second, third in tap_list()
        ],
        axis=2,
    )
    flat_kernel = kernel.reshape(-1, chans_total)
    terms = jnp.einsum("kc,xykz->xycz", flat_kernel, stacked, preferred_element_type=jnp.float32)
    input_grad = lax.psum_scatter(terms, "chan", scatter_dimension=2, tiled=True).astype(
        jnp.bfloat16
    )
    return (output, input_grad, weight_grad)


def solution(mesh):
    return jax.shard_map(
        on_device,
        mesh=mesh,
        in_specs=(
            P("space", None, "chan", None),
            P(None, "chan", None),
            P("chan"),
            P("space", None, "chan", None),
        ),
        out_specs=(
            P("space", None, "chan", None),
            P("space", None, "chan", None),
            P(None, "chan", None),
        ),
        check_vma=False,
    )
```

profile of v0, /device:TPU:0, one launch (start us, length us, event | category | flops | bytes accessed | tf_op | source)
XLA Modules:
  0.0 400.5 jit_solution(16607574144106537351)
XLA Ops:
  7.9 57.2 %all-gather.2.cloned.1.call-done = bf16[4,16,256,128]{3,2,1,0:T(8,128)(2,1)} async-done(((bf16[4,16,64,128]{3,2,1,0:T(8,128)(2,1)}), bf16[4,16,256,128]{3,2,1,0:T(8,128)(2,1)}) %all-gather.2.cloned.1.call-update) | async-done | bytes 4194320 | tf_op jit(solution)/shard_map/all_gather | solution.py:39
  65.2 1.8 fusion.325
  67.0 1.8 collective-permute-start
  70.1 1.6 fusion.279
  71.7 3.0 collective-permute-done.1
  74.7 12.5 %select_maximum_fusion = bf16[6,18,256,130]{3,2,1,0:T(8,128)(2,1)S(1)} fusion(bf16[1,16,256,128]{3,2,1,0:T(8,128)(2,1)S(1)} %collective-permute-done.1, bf16[4,16,256,128]{3,2,1,0:T(8,128)(2,1)S(1)} %copy-done, bf16[1,16,256,128]{3,2,1,0:T(8,128)(2,1)S(1)} %collective-permute-done), kind=kLoop, calls=%fused_computation.7 | loop fusion | flops 68290560 | bytes 13479936 | tf_op jit(solution)/shard_map/concatenate | solution.py:15
  87.2 3.0 fusion.15
  90.2 2.2 fusion.19
  92.4 3.0 fusion.23
  95.4 2.2 fusion.27
  97.7 3.0 fusion.31
  100.7 3.0 fusion.35
  103.7 2.2 fusion.39
  105.8 3.0 fusion.43
  108.8 3.0 fusion.47
  111.8 2.2 fusion.51
  114.0 3.4 fusion.55
  117.4 2.2 fusion.59
  119.7 3.0 fusion.63
  122.7 3.0 fusion.67
  125.7 2.2 fusion.71
  127.8 3.0 fusion.75
  130.8 3.0 fusion.79
  133.9 2.2 fusion.83
  136.0 3.0 fusion.87
  139.0 2.2 fusion.91
  141.2 3.2 fusion.95
  144.4 3.0 fusion.99
  147.3 2.2 fusion.103
  149.5 2.2 fusion.110
  151.7 2.2 fusion.108
  154.0 18.7 %multiply_convert_fusion = (bf16[4,16,64,128]{3,2,1,0:T(8,128)(2,1)S(1)}, bf16[4,16,64,128]{3,2,1,0:T(8,128)(2,1)}) fusion(bf16[4,16,64,128]{3,2,1,0:T(8,128)(2,1)} %param.7, f32[64]{0:T(128)S(1)} %copy-done.9, bf16[6,18,256,130]{3,2,1,0:T(8,128)(2,1)S(1)} %select_maximum_fusion, bf16[27,64,256]{2,1,0:T(8,128)(2,1)} %param.5, ...), kind=kOutput, calls=%fused_computation.138 | convolution fusion | flops 288882688 | bytes 61899264 | tf_op jit(solution)/shard_map/oc,xycz->xyoz/dot_general | solution.py:46
  174.9 14.0 %collective-permute-start.2 = (bf16[1,16,64,128]{3,2,1,0:T(8,128)(2,1)}, bf16[1,16,64,128]{3,2,1,0:T(8,128)(2,1)S(1)}, u32[]{:S(2)}, u32[]{:S(2)}) collective-permute-start(bf16[1,16,64,128]{3,2,1,0:T(8,128)(2,1)} %get-tuple-element.13), channel_id=1, source_target_pairs={{0,1},{1,2},{2,3},{3,4},{4,5},{5,6},{6,7},{8,9},{9,10},{10,11},{11... | collective-permute-start | bytes 786440 | tf_op jit(solution)/shard_map/ppermute | solution.py:17
  190.1 2.0 fusion.128
  192.2 2.0 fusion.134
  195.6 1.4 fusion.118
  197.0 2.0 fusion.146
  199.0 1.4 fusion.152
  200.4 2.0 fusion.158
  202.4 2.0 fusion.164
  204.4 1.4 fusion.170
  205.8 2.4 fusion.176
  208.2 2.0 fusion.182
  211.6 1.4 fusion.263
  213.0 2.0 fusion.194
  216.4 2.0 fusion.206
  218.4 2.0 fusion.212
  220.4 1.4 fusion.218
  221.8 2.0 fusion.224
  223.8 2.2 fusion.230
  226.0 1.4 fusion.236
  227.4 1.4 fusion.116
  228.8 2.0 fusion.242
  232.2 2.0 fusion.254
  234.2 2.0 fusion.260
  237.7 3.2 select_maximum_fusion.2
  252.7 9.6 %copy-done.1 = bf16[4,16,1728,128]{3,2,1,0:T(8,128)(2,1)} copy-done((bf16[4,16,1728,128]{3,2,1,0:T(8,128)(2,1)}, bf16[4,16,1728,128]{3,2,1,0:T(8,128)(2,1)S(1)}, u32[]{:S(2)}) %copy-start.1) | copy-done | bytes 28311576
  262.3 15.5 %convolution_bitcast_fusion = f32[4,16,256,128]{2,3,1,0:T(8,128)} fusion(bf16[4,16,1728,128]{3,2,1,0:T(8,128)(2,1)} %copy-done.1, bf16[1728,256,1,1]{1,0,3,2:T(8,128)(2,1)S(1)} %bitcast.487), kind=kOutput, calls=%fused_computation.122 | convolution fusion | flops 7247757312 | bytes 37584896 | tf_op jit(solution)/shard_map/kc,xykz->xycz/dot_general | solution.py:78
  277.8 10.3 %copy.8 = f32[4,16,256,128]{3,1,0,2:T(8,128)} copy(f32[4,16,256,128]{2,3,1,0:T(8,128)} %convolution_bitcast_fusion) | data formatting | bytes 16777216 | tf_op jit(solution)/shard_map/kc,xykz->xycz/transpose | solution.py:78
  288.2 13.4 %all-reduce.4.cloned.1.call-done = f32[27,64,256]{2,1,0:T(8,128)} async-done(((f32[27,64,256]{2,1,0:T(8,128)}), f32[27,64,256]{2,1,0:T(8,128)}) %all-reduce.4.cloned.1.call-update) | async-done | bytes 1769488 | tf_op jit(solution)/shard_map/psum | solution.py:61
  301.6 2.9 broadcast_multiply_fusion
  304.4 85.8 %reduce-scatter.2.cloned.1.call-done = f32[4,16,64,128]{3,1,0,2:T(8,128)} async-done(((f32[4,16,256,128]{3,1,0,2:T(8,128)}), f32[4,16,64,128]{3,1,0,2:T(8,128)}) %reduce-scatter.2.cloned.1.call-update) | async-done | bytes 2097168 | tf_op jit(solution)/shard_map/reduce_scatter | solution.py:79
  390.3 1.8 convert_element_type.19
  392.1 1.6 copy.9
  (63 shorter events, 24.2 us)
Async XLA Ops:
  7.2 58.0 %all-gather.2.cloned.1.call-start = ((), (), s32[]{:S(2)}) async-start(), calls=%async_computation.1 | async-start | bytes 5242880 | tf_op jit(solution)/shard_map/all_gather | solution.py:39
  7.9 293.7 %all-reduce.4.cloned.1.call-start = ((), (), s32[]{:S(2)}) async-start(), calls=%async_computation.3 | async-start | bytes 3538944 | tf_op jit(solution)/shard_map/psum | solution.py:61
  65.2 4.9 %copy-start = (bf16[4,16,256,128]{3,2,1,0:T(8,128)(2,1)S(1)}, bf16[4,16,256,128]{3,2,1,0:T(8,128)(2,1)}, u32[]{:S(2)}) copy-start(bf16[4,16,256,128]{3,2,1,0:T(8,128)(2,1)} %all-gather.2.cloned.1.call-done) | copy-start | bytes 12582916
  67.0 4.7 %collective-permute-start = (bf16[1,16,256,128]{3,2,1,0:T(8,128)(2,1)S(1)}, bf16[1,16,256,128]{3,2,1,0:T(8,128)(2,1)S(1)}, u32[]{:S(2)}, u32[]{:S(2)}) collective-permute-start(bf16[1,16,256,128]{3,2,1,0:T(8,128)(2,1)S(1)} %get-tuple-element.9), channel_id=1, source_target_pairs={{0,1},{1,2},{2,3},{3,4},{4,5},{5,6},{6,7},{8,9},{9,10},{10,11},{11... | collective-permute-start | bytes 3145736 | tf_op jit(solution)/shard_map/ppermute | solution.py:17
  68.8 5.9 %collective-permute-start.1 = (bf16[1,16,256,128]{3,2,1,0:T(8,128)(2,1)S(1)}, bf16[1,16,256,128]{3,2,1,0:T(8,128)(2,1)S(1)}, u32[]{:S(2)}, u32[]{:S(2)}) collective-permute-start(bf16[1,16,256,128]{3,2,1,0:T(8,128)(2,1)S(1)} %get-tuple-element.10), channel_id=1, source_target_pairs={{1,0},{2,1},{3,2},{4,3},{5,4},{6,5},{7,6},{9,8},{10,9},{11,10},{12... | collective-permute-start | bytes 3145736 | tf_op jit(solution)/shard_map/ppermute | solution.py:19
  71.7 15.5 %copy-start.6 = (bf16[27,64,256]{2,1,0:T(8,128)(2,1)S(1)}, bf16[27,64,256]{2,1,0:T(8,128)(2,1)}, u32[]{:S(2)}) copy-start(bf16[27,64,256]{2,1,0:T(8,128)(2,1)} %param.5) | copy-start | bytes 2654212
  71.7 80.0 %copy-start.4 = (bf16[1,16,256,128]{3,2,1,0:T(8,128)(2,1)}, bf16[1,16,256,128]{3,2,1,0:T(8,128)(2,1)S(1)}, u32[]{:S(2)}) copy-start(bf16[1,16,256,128]{3,2,1,0:T(8,128)(2,1)S(1)} %collective-permute-done) | copy-start | bytes 3145732
  74.7 74.8 %copy-start.2 = (bf16[1,16,256,128]{3,2,1,0:T(8,128)(2,1)}, bf16[1,16,256,128]{3,2,1,0:T(8,128)(2,1)S(1)}, u32[]{:S(2)}) copy-start(bf16[1,16,256,128]{3,2,1,0:T(8,128)(2,1)S(1)} %collective-permute-done.1) | copy-start | bytes 3145732
  151.7 2.2 copy-start.9
  174.9 62.9 %collective-permute-start.2 = (bf16[1,16,64,128]{3,2,1,0:T(8,128)(2,1)}, bf16[1,16,64,128]{3,2,1,0:T(8,128)(2,1)S(1)}, u32[]{:S(2)}, u32[]{:S(2)}) collective-permute-start(bf16[1,16,64,128]{3,2,1,0:T(8,128)(2,1)} %get-tuple-element.13), channel_id=1, source_target_pairs={{0,1},{1,2},{2,3},{3,4},{4,5},{5,6},{6,7},{8,9},{9,10},{10,11},{11... | collective-permute-start | bytes 786440 | tf_op jit(solution)/shard_map/ppermute | solution.py:17
  188.8 48.9 %collective-permute-start.3 = (bf16[1,16,64,128]{3,2,1,0:T(8,128)(2,1)}, bf16[1,16,64,128]{3,2,1,0:T(8,128)(2,1)S(1)}, u32[]{:S(2)}, u32[]{:S(2)}) collective-permute-start(bf16[1,16,64,128]{3,2,1,0:T(8,128)(2,1)} %get-tuple-element.14), channel_id=1, source_target_pairs={{1,0},{2,1},{3,2},{4,3},{5,4},{6,5},{7,6},{9,8},{10,9},{11,10},{12... | collective-permute-start | bytes 786440 | tf_op jit(solution)/shard_map/ppermute | solution.py:19
  194.2 1.4 copy-start.5
  226.0 1.4 copy-start.3
  236.2 1.2 copy-start.8
  237.4 152.8 %reduce-scatter.2.cloned.1.call-start = ((), (), s32[]{:S(2)}) async-start(), calls=%async_computation.2 | async-start | bytes 10485760 | tf_op jit(solution)/shard_map/reduce_scatter | solution.py:79
  250.9 11.4 %copy-start.7 = (bf16[27,64,256]{2,1,0:T(8,128)(2,1)S(1)}, bf16[27,64,256]{2,1,0:T(8,128)(2,1)}, u32[]{:S(2)}) copy-start(bf16[27,64,256]{2,1,0:T(8,128)(2,1)} %param.5) | copy-start | bytes 2654212
  252.7 9.6 %copy-start.1 = (bf16[4,16,1728,128]{3,2,1,0:T(8,128)(2,1)}, bf16[4,16,1728,128]{3,2,1,0:T(8,128)(2,1)S(1)}, u32[]{:S(2)}) copy-start(bf16[4,16,1728,128]{3,2,1,0:T(8,128)(2,1)S(1)} %slice_dynamic-update-slice_fusion) | copy-start | bytes 84934656
Sparse Core Ops, SparseCore 0:
  9.8 55.2 all-gather.1
  237.6 63.9 all-reduce.3
  304.6 85.5 reduce-scatter.1
where the time goes:
time: 404 us; the launch traced here: 401 us
  waiting for transfers between devices  160 us (40%)
  matrix products  150 us (37%)
  local copies, waits for them, and re-layouts  36.8 us (9%)
  other arithmetic  20.6 us (5%)
  starting transfers between devices  18.7 us (5%)
  between operations  14.5 us (4%)
    dot_general x27, matrix products, on_device(): jnp.einsum('oc,xycz->xyoz', kernel[index_tap], slab, preferred_element_ty...  87 us
    reduce_scatter x1, waiting for transfers between devices, on_device(): lax.psum_scatter(terms, 'chan', scatter_dimension=2, tiled=True)  85.8 us
    all_gather x1, waiting for transfers between devices, on_device(): whole_chans = lax.all_gather(volume, 'chan', axis=2, tiled=True)  57.2 us
    dot_general x27, matrix products, on_device(): jnp.einsum('xyoz,xycz->oc', grad_pre, slab, preferred_element_type=jnp.fl...  47.3 us
    unnamed x45, local copies, waits for them, and re-layouts  23.5 us
    ppermute x2, starting transfers between devices, padded_2(): lax.ppermute(tail, axis, [(i, (i + 1) % count) for i in range(ends)])  15.7 us
    concatenate x2, other arithmetic, padded_2(): jnp.concatenate([lax.ppermute(tail, axis, [(i, (i + 1) % count) for i in...  15.7 us
    dot_general x1, matrix products, on_device(): jnp.einsum('kc,xykz->xycz', flat_kernel, stacked, preferred_element_type=...  15.5 us
  transfers between devices with their start and end apart: 7, of which 4 were waited for; matrix products, arithmetic and copies ran while one was open for 23% of the time, Pallas kernels for 0%

commit v1 on v0

v1 whole, which is shorter than its diff:
```python
import functools
import math

import jax
import jax.numpy as jnp
from jax import lax
from jax.experimental import pallas as pl
from jax.experimental.pallas import tpu as pltpu
from jax.sharding import PartitionSpec as P

F32 = jnp.float32
BF16 = jnp.bfloat16
VMEM_LIMIT = 60 * 1024 * 1024


def shifted(rows, amount):
    size_z = rows.shape[1]
    lane = lax.broadcasted_iota(jnp.int32, rows.shape, 1)
    edge = 0 if amount == 1 else size_z - 1
    return jnp.where(lane == edge, 0.0, pltpu.roll(rows, amount % size_z, 1))


def lay_out(lo_ref, mid_ref, hi_ref, planes):
    size_x, size_y, chans, size_z = mid_ref.shape
    edge = jnp.zeros(((size_x + 2) * chans, size_z), BF16)
    planes[:, 0:size_z] = edge
    planes[:, (size_y + 1) * size_z : (size_y + 2) * size_z] = edge
    for y in range(size_y):
        lanes = slice((y + 1) * size_z, (y + 2) * size_z)
        planes[0:chans, lanes] = lo_ref[0, y]
        planes[(size_x + 1) * chans : (size_x + 2) * chans, lanes] = hi_ref[0, y]

        def put(x, _, y=y, lanes=lanes):
            planes[pl.ds((x + 1) * chans, chans), lanes] = mid_ref[x, y]
            return 0

        lax.fori_loop(0, size_x, put, 0)


def conv_rows(planes, w_ref, chans, size_z, x, y, count):
    total = None
    for dy in range(3):
        lanes = pl.ds(pl.multiple_of((y + dy) * size_z, size_z), count * size_z)
        cells = planes[pl.ds(pl.multiple_of(x * chans, chans), 3 * chans), lanes]
        part = jnp.dot(w_ref[dy], cells, preferred_element_type=F32)
        total = part if total is None else total + part
    return total


def tap_sum(total, outs, size_z, row):
    lanes = slice(row * size_z, (row + 1) * size_z)
    return (
        total[outs : 2 * outs, lanes]
        + shifted(total[0:outs, lanes], 1)
        + shifted(total[2 * outs : 3 * outs, lanes], -1)
    )


def forward_kernel(lo_ref, mid_ref, hi_ref, w_ref, bias_ref, cot_ref, out_ref, grad_ref, three_ref, planes):
    size_x, size_y, chans, size_z = mid_ref.shape
    outs = cot_ref.shape[2]
    lay_out(lo_ref, mid_ref, hi_ref, planes)
    count = 2

    def step(index, _):
        x = index // (size_y // count)
        y = (index % (size_y // count)) * count
        total = conv_rows(planes, w_ref, chans, size_z, x, y, count)
        for row in range(count):
            pre = tap_sum(total, outs, size_z, row) + bias_ref[...]
            sig = jax.nn.sigmoid(pre)
            out_ref[x, y + row] = (pre * sig).astype(BF16)
            grad = cot_ref[x, y + row].astype(F32) * sig * (1.0 + pre * (1.0 - sig))
            held = grad.astype(BF16)
            grad_ref[x, y + row] = held
            grad = held.astype(F32)
            lanes = pl.ds(pl.multiple_of((y + row) * size_z, size_z), size_z)
            three_ref[x, 0:outs, lanes] = shifted(grad, -1).astype(BF16)
            three_ref[x, outs : 2 * outs, lanes] = held
            three_ref[x, 2 * outs : 3 * outs, lanes] = shifted(grad, 1).astype(BF16)
        return 0

    lax.fori_loop(0, size_x * size_y // count, step, 0)


def weight_kernel(three_ref, planes, acc_ref):
    size_x, _, cells = three_ref.shape
    wide = acc_ref.shape[2]
    chans = wide // 3
    size_z = (planes.shape[1] - cells) // 2
    acc_ref[...] = jnp.zeros_like(acc_ref)

    def step(x, _):
        for dy in range(3):
            cube = planes[pl.ds(pl.multiple_of(x * chans, chans), wide), dy * size_z : dy * size_z + cells]
            acc_ref[dy] += lax.dot_general(
                three_ref[x], cube, (((1,), (1,)), ((), ())), preferred_element_type=F32
            )
        return 0

    lax.fori_loop(0, size_x, step, 0)


def input_kernel(lo_ref, mid_ref, hi_ref, w_ref, out_ref, planes):
    size_x, size_y, chans, size_z = mid_ref.shape
    outs = out_ref.shape[2]
    lay_out(lo_ref, mid_ref, hi_ref, planes)
    count = 2

    def step(index, _):
        x = index // (size_y // count)
        y = (index % (size_y // count)) * count
        total = conv_rows(planes, w_ref, chans, size_z, x, y, count)
        for row in range(count):
            out_ref[x, y + row] = tap_sum(total, outs, size_z, row).astype(BF16)
        return 0

    lax.fori_loop(0, size_x * size_y // count, step, 0)


def call(kernel, args, outs, scratch, flops):
    whole = pl.BlockSpec(memory_space=pltpu.VMEM)
    size = sum(a.size * a.dtype.itemsize for a in args)
    return pl.pallas_call(
        kernel,
        out_shape=outs,
        in_specs=[whole] * len(args),
        out_specs=jax.tree.map(lambda _: whole, outs),
        scratch_shapes=scratch,
        compiler_params=pltpu.CompilerParams(vmem_limit_bytes=VMEM_LIMIT),
        cost_estimate=pl.CostEstimate(flops=flops, bytes_accessed=size, transcendentals=0),
    )(*args)


def with_neighbours(cells):
    count = lax.axis_size("space")
    up = [(i, i + 1) for i in range(count - 1)]
    down = [(i + 1, i) for i in range(count - 1)]
    lo = lax.ppermute(cells[-1:], "space", up)
    hi = lax.ppermute(cells[:1], "space", down)
    return lo, cells, hi


def on_device(volume, kernel, bias, cotangent):
    size_x, size_y, chans_local, size_z = volume.shape
    taps, outs, chans = kernel.shape
    shape = jax.ShapeDtypeStruct
    flops = 2 * size_x * size_y * size_z * taps * outs * chans
    cube = kernel.reshape(3, 3, 3, outs, chans)
    w_forward = cube.transpose(1, 2, 3, 0, 4).reshape(3, 3 * outs, 3 * chans)
    turned = lax.all_to_all(kernel, "chan", split_axis=2, concat_axis=1, tiled=True)
    all_outs, ins = turned.shape[1], turned.shape[2]
    turned = turned.reshape(3, 3, 3, all_outs, ins)[::-1, ::-1, ::-1]
    w_input = turned.transpose(1, 2, 4, 0, 3).reshape(3, 3 * ins, 3 * all_outs)
    column = jnp.broadcast_to(bias.reshape(outs, 1), (outs, size_z))

    padded = (size_y + 2) * size_z
    gathered = lax.all_gather(volume, "chan", axis=2, tiled=True)
    output, grad_pre, three, planes = call(
        forward_kernel,
        (*with_neighbours(gathered), w_forward, column, cotangent),
        (
            shape(cotangent.shape, BF16),
            shape(cotangent.shape, BF16),
            shape((size_x, 3 * outs, size_y * size_z), BF16),
            shape(((size_x + 2) * chans, padded), BF16),
        ),
        [],
        flops,
    )
    grads = lax.all_gather(grad_pre, "chan", axis=2, tiled=True)
    partial = call(weight_kernel, (three, planes), shape((3, 3 * outs, 3 * chans), F32), [], flops)
    summed = lax.psum(partial, "space") / math.sqrt(size_x * size_y * size_z * lax.axis_size("space"))
    weight_grad = summed.reshape(3, 3, outs, 3, chans).transpose(3, 0, 1, 2, 4).reshape(taps, outs, chans)
    input_grad = call(
        input_kernel,
        (*with_neighbours(grads), w_input),
        shape(volume.shape, BF16),
        [pltpu.VMEM(((size_x + 2) * all_outs, padded), BF16)],
        flops,
    )
    return output, input_grad, weight_grad


def solution(mesh):
    return jax.shard_map(
        on_device,
        mesh=mesh,
        in_specs=(
            P("space", None, "chan", None),
            P(None, "chan", None),
            P("chan"),
            P("space", None, "chan", None),
        ),
        out_specs=(
            P("space", None, "chan", None),
            P("space", None, "chan", None),
            P(None, "chan", None),
        ),
        check_vma=False,
    )
```

time: 404 us -> 281 us (0.70)
  matrix products: 150 us -> 0 us
  Pallas kernels: 0 us -> 68.1 us
  other arithmetic: 20.6 us -> 2.82 us
  waiting for transfers between devices: 160 us -> 152 us
  local copies, waits for them, and re-layouts: 36.8 us -> 29.6 us
  starting transfers between devices: 18.7 us -> 14.2 us
    dot_general x55 -> x0, matrix products: 150 us -> none  [the longest x27 87 us: on_device(): jnp.einsum('oc,xycz->xyoz', kernel[index_tap], slab, preferred_element_ty...]
    reduce_scatter x1 -> x0, waiting for transfers between devices: 85.8 us -> none  [on_device(): lax.psum_scatter(terms, 'chan', scatter_dimension=2, tiled=True)]
    pallas_call x0 -> x3, Pallas kernels: none -> 68.1 us  [call(): pl.pallas_call(kernel, out_shape=outs, in_specs=[whole] * len(args), out_...]
    all_gather x1 -> x2, waiting for transfers between devices: 57.2 us -> 101 us  [the longest x1 57.2 us: on_device(): gathered = lax.all_gather(volume, 'chan', axis=2, tiled=True)]
    psum x1, waiting for transfers between devices: 13.4 us -> 50.1 us  [on_device(): lax.psum(partial, 'space')]
    unnamed x45 -> x7, local copies, waits for them, and re-layouts: 23.5 us -> 7.28 us
    concatenate x2 -> x0, other arithmetic: 15.7 us -> none  [padded_2(): jnp.concatenate([lax.ppermute(tail, axis, [(i, (i + 1) % count) for i in...]
    reshape x0 -> x5, local copies, waits for them, and re-layouts: none -> 10.8 us  [the longest x1 3.08 us: on_device(): turned = turned.reshape(3, 3, 3, all_outs, ins)[::-1, ::-1, ::-1]]
  transfers between devices with their start and end apart: 7 -> 8, of which waited for: 4 -> 3; matrix products, arithmetic and copies ran while one was open for 23% -> 10% of each run, Pallas kernels for 0% -> 6%
where the time goes in v1:
time: 281 us; the launch traced here: 280 us
  waiting for transfers between devices  152 us (54%)
  Pallas kernels  68.1 us (24%)
  local copies, waits for them, and re-layouts  29.6 us (11%)
  starting transfers between devices  14.2 us (5%)
  between operations  13.8 us (5%)
  other arithmetic  2.82 us (1%)
    pallas_call x3, Pallas kernels, call(): pl.pallas_call(kernel, out_shape=outs, in_specs=[whole] * len(args), out_...  68.1 us
    all_gather x1, waiting for transfers between devices, on_device(): gathered = lax.all_gather(volume, 'chan', axis=2, tiled=True)  57.2 us
    psum x1, waiting for transfers between devices, on_device(): lax.psum(partial, 'space')  50.1 us
    all_gather x1, waiting for transfers between devices, on_device(): grads = lax.all_gather(grad_pre, 'chan', axis=2, tiled=True)  43.7 us
    ppermute x2, starting transfers between devices, with_neighbours(): lo = lax.ppermute(cells[-1:], 'space', up)  8.05 us
    unnamed x7, local copies, waits for them, and re-layouts  7.28 us
    slice x2, local copies, waits for them, and re-layouts, with_neighbours(): hi = lax.ppermute(cells[:1], 'space', down)  5.81 us
  transfers between devices with their start and end apart: 8, of which 3 were waited for; matrix products, arithmetic and copies ran while one was open for 10% of the time, Pallas kernels for 6%

profile of v1, /device:TPU:0, one launch (start us, length us, event | category | flops | bytes accessed | tf_op | source)
XLA Modules:
  0.0 280.3 jit_solution(13176960351870392234)
XLA Ops:
  7.2 0.0 all-gather.3.cloned.1.call-start
  7.2 0.7 all-gather.3.cloned.1.call-update
  7.9 0.0 copy-start
  7.9 0.0 all-gather.5.cloned.1.call-start
  8.0 57.2 %all-gather.3.cloned.1.call-done.mid_ref = bf16[4,16,256,128]{3,2,1,0:T(8,128)(2,1)} async-done(((bf16[4,16,64,128]{3,2,1,0:T(8,128)(2,1)}), bf16[4,16,256,128]{3,2,1,0:T(8,128)(2,1)}) %all-gather.3.cloned.1.call-update) | async-done | bytes 4194320 | tf_op jit(solution)/shard_map/all_gather | solution.py:158
  65.1 2.7 fusion.1
  67.8 1.3 collective-permute-start.1
  69.1 4.0 %collective-permute-start = (bf16[1,16,256,128]{3,2,1,0:T(8,128)(2,1)S(1)}, bf16[1,16,256,128]{3,2,1,0:T(8,128)(2,1)}, u32[]{:S(2)}, u32[]{:S(2)}) collective-permute-start(bf16[1,16,256,128]{3,2,1,0:T(8,128)(2,1)S(1)} %get-tuple-element.14), channel_id=1, source_target_pairs={{0,1},{1,2},{2,3},{3,4},{4,5},{5,6},{6,7},{8,9},{9,10},{10,11},{11... | collective-permute-start | bytes 3145736 | tf_op jit(solution)/shard_map/ppermute | solution.py:139
  73.2 0.0 copy-done
  73.2 0.0 copy-start.1
  73.2 0.8 copy.24
  73.9 2.1 reshape.28.w_ref
  76.1 0.0 collective-permute-done.1.hi_ref
  76.1 0.0 collective-permute-done.lo_ref
  76.1 0.0 copy-done.1
  76.1 0.7 broadcast_in_dim.2.bias_ref
  76.7 28.6 %shard_map.67 = (bf16[4,16,64,128]{3,2,1,0:T(8,128)(2,1)}, bf16[4,16,64,128]{3,2,1,0:T(8,128)(2,1)}, bf16[4,192,2048]{2,1,0:T(8,128)(2,1)}, bf16[1536,2304]{1,0:T(8,128)(2,1)}) custom-call(bf16[1,16,256,128]{3,2,1,0:T(8,128)(2,1)} %collective-permute-done.lo_ref, bf16[4,16,256,128]{3,2,1,0:T(8,128)(2,1)} %all-gather.3.cloned.1.call-done.mid_ref, ...), custom_call_target="tpu_custom_call" | custom-call | flops 7247757312 | bytes 8257536 | tf_op jit(solution)/shard_map/pallas_call | solution.py:124
  105.3 0.0 all-gather.5.cloned.1.call-update
  105.4 3.1 %copy.17 = bf16[27,64,256]{1,0,2:T(8,128)(2,1)S(1)} copy(bf16[27,64,256]{2,1,0:T(8,128)(2,1)S(1)} %copy-done) | data formatting | bytes 1769472 | tf_op args[1]
  108.4 2.4 reshape.33
  110.8 3.5 %all-to-all-start = ((bf16[4,2,55296]{2,1,0:T(2,128)(2,1)}), bf16[4,2,55296]{2,1,0:T(2,128)(2,1)S(1)}, u32[]{:S(2)}, u32[]{:S(2)}) async-start(bf16[4,2,55296]{2,1,0:T(2,128)(2,1)} %reshape.33), calls=%async_computation | async-start | bytes 1769472 | tf_op jit(solution)/shard_map/all_to_all | solution.py:151
  114.3 0.0 all-reduce.2.cloned.1.call-start
  114.4 18.0 %shard_map.69 = f32[3,192,768]{2,1,0:T(8,128)} custom-call(bf16[4,192,2048]{2,1,0:T(8,128)(2,1)} %get-tuple-element.9.three_ref, bf16[1536,2304]{1,0:T(8,128)(2,1)} %get-tuple-element.10.planes), custom_call_target="tpu_custom_call" | custom-call | flops 7247757312 | bytes 10223616 | tf_op jit(solution)/shard_map/pallas_call | solution.py:124
  132.4 0.0 all-reduce.2.cloned.1.call-update
  132.5 43.7 %all-gather.5.cloned.1.call-done.mid_ref = bf16[4,16,256,128]{3,2,1,0:T(8,128)(2,1)} async-done(((bf16[4,16,64,128]{3,2,1,0:T(8,128)(2,1)}), bf16[4,16,256,128]{3,2,1,0:T(8,128)(2,1)}) %all-gather.5.cloned.1.call-update) | async-done | bytes 4194320 | tf_op jit(solution)/shard_map/all_gather | solution.py:171
  176.2 3.1 %fusion = (bf16[1,16,256,128]{3,2,1,0:T(8,128)(2,1)}, bf16[1,16,256,128]{3,2,1,0:T(8,128)(2,1)}) fusion(bf16[4,16,256,128]{3,2,1,0:T(8,128)(2,1)} %all-gather.5.cloned.1.call-done.mid_ref), kind=kLoop, calls=%fused_computation.4 | loop fusion | bytes 4194304 | tf_op jit(solution)/shard_map/slice | solution.py:140
  179.3 1.3 collective-permute-start.3
  180.6 4.0 %collective-permute-start.2 = (bf16[1,16,256,128]{3,2,1,0:T(8,128)(2,1)}, bf16[1,16,256,128]{3,2,1,0:T(8,128)(2,1)}, u32[]{:S(2)}, u32[]{:S(2)}) collective-permute-start(bf16[1,16,256,128]{3,2,1,0:T(8,128)(2,1)} %get-tuple-element.12), channel_id=1, source_target_pairs={{0,1},{1,2},{2,3},{3,4},{4,5},{5,6},{6,7},{8,9},{9,10},{10,11},{11... | collective-permute-start | bytes 3145736 | tf_op jit(solution)/shard_map/ppermute | solution.py:139
  184.6 0.0 all-to-all-done
  184.6 1.8 reshape.34
  186.5 2.6 copy.23
  189.1 3.1 %reshape.29 = bf16[3,3,3,256,64]{3,4,2,1,0:T(8,128)(2,1)S(1)} reshape(bf16[27,4,64,64]{2,1,3,0:T(4,128)(2,1)} %bitcast.19) | data formatting | bytes 1769472 | tf_op jit(solution)/shard_map/reshape | solution.py:153
  192.2 0.1 reverse_bitcast_fusion
  192.2 0.8 copy.19
  193.0 2.1 reshape.30.w_ref
  195.1 50.1 %all-reduce.2.cloned.1.call-done = f32[3,192,768]{2,1,0:T(8,128)} async-done(((f32[3,192,768]{2,1,0:T(8,128)}), f32[3,192,768]{2,1,0:T(8,128)}) %all-reduce.2.cloned.1.call-update) | async-done | bytes 1769488 | tf_op jit(solution)/shard_map/psum | solution.py:173
  245.2 2.8 %broadcast_multiply_fusion = f32[3,192,768]{2,1,0:T(8,128)} fusion(f32[3,192,768]{2,1,0:T(8,128)} %all-reduce.2.cloned.1.call-done), kind=kLoop, calls=%fused_computation.2 | loop fusion | flops 442368 | bytes 3538944 | tf_op jit(solution)/shard_map/div | solution.py:173
  248.0 2.7 reshape.31
  250.8 1.5 copy.20
  252.3 0.0 collective-permute-done.3.hi_ref
  252.3 0.0 collective-permute-done.2.lo_ref
  252.3 21.4 %shard_map.68 = bf16[4,16,64,128]{3,2,1,0:T(8,128)(2,1)} custom-call(bf16[1,16,256,128]{3,2,1,0:T(8,128)(2,1)} %collective-permute-done.2.lo_ref, bf16[4,16,256,128]{3,2,1,0:T(8,128)(2,1)} %all-gather.5.cloned.1.call-done.mid_ref, bf16[1,16,256,128]{3,2,1,0:T(8,128)(2,1)} %collective-permute-done.3.hi_ref, bf16[3,192,768]{2,1,0:T(8,128)(2,1)} %reshape.30.w_ref), custom_call_target="tpu_custom_call" | custom-call | flops 7247757312 | bytes 7176192 | tf_op jit(solution)/shard_map/pallas_call | solution.py:124
Async XLA Ops:
  7.2 58.0 %all-gather.3.cloned.1.call-start = ((), (), s32[]{:S(2)}) async-start(), calls=%async_computation.1 | async-start | bytes 5242880 | tf_op jit(solution)/shard_map/all_gather | solution.py:158
  7.9 65.3 %copy-start = (bf16[27,64,256]{2,1,0:T(8,128)(2,1)S(1)}, bf16[27,64,256]{2,1,0:T(8,128)(2,1)}, u32[]{:S(2)}) copy-start(bf16[27,64,256]{2,1,0:T(8,128)(2,1)} %param.5) | copy-start | bytes 2654212
  7.9 168.3 %all-gather.5.cloned.1.call-start = ((), (), s32[]{:S(2)}) async-start(), calls=%async_computation.2 | async-start | bytes 5242880 | tf_op jit(solution)/shard_map/all_gather | solution.py:171
  67.8 8.2 %collective-permute-start.1 = (bf16[1,16,256,128]{3,2,1,0:T(8,128)(2,1)}, bf16[1,16,256,128]{3,2,1,0:T(8,128)(2,1)}, u32[]{:S(2)}, u32[]{:S(2)}) collective-permute-start(bf16[1,16,256,128]{3,2,1,0:T(8,128)(2,1)} %get-tuple-element.13), channel_id=1, source_target_pairs={{1,0},{2,1},{3,2},{4,3},{5,4},{6,5},{7,6},{9,8},{10,9},{11,10},{12... | collective-permute-start | bytes 3145736 | tf_op jit(solution)/shard_map/ppermute | solution.py:140
  69.1 6.9 %collective-permute-start = (bf16[1,16,256,128]{3,2,1,0:T(8,128)(2,1)S(1)}, bf16[1,16,256,128]{3,2,1,0:T(8,128)(2,1)}, u32[]{:S(2)}, u32[]{:S(2)}) collective-permute-start(bf16[1,16,256,128]{3,2,1,0:T(8,128)(2,1)S(1)} %get-tuple-element.14), channel_id=1, source_target_pairs={{0,1},{1,2},{2,3},{3,4},{4,5},{5,6},{6,7},{8,9},{9,10},{10,11},{11... | collective-permute-start | bytes 3145736 | tf_op jit(solution)/shard_map/ppermute | solution.py:139
  73.2 2.9 %copy-start.1 = (f32[64]{0:T(128)S(1)}, f32[64]{0:T(128)}, u32[]{:S(2)}) copy-start(f32[64]{0:T(128)} %param.6) | copy-start | bytes 772
  110.8 73.8 %all-to-all-start = ((bf16[4,2,55296]{2,1,0:T(2,128)(2,1)}), bf16[4,2,55296]{2,1,0:T(2,128)(2,1)S(1)}, u32[]{:S(2)}, u32[]{:S(2)}) async-start(bf16[4,2,55296]{2,1,0:T(2,128)(2,1)} %reshape.33), calls=%async_computation | async-start | bytes 1769472 | tf_op jit(solution)/shard_map/all_to_all | solution.py:151
  114.3 130.9 %all-reduce.2.cloned.1.call-start = ((), (), s32[]{:S(2)}) async-start(), calls=%async_computation.3 | async-start | bytes 3538944 | tf_op jit(solution)/shard_map/psum | solution.py:173
  179.3 73.0 %collective-permute-start.3 = (bf16[1,16,256,128]{3,2,1,0:T(8,128)(2,1)}, bf16[1,16,256,128]{3,2,1,0:T(8,128)(2,1)}, u32[]{:S(2)}, u32[]{:S(2)}) collective-permute-start(bf16[1,16,256,128]{3,2,1,0:T(8,128)(2,1)} %get-tuple-element.11), channel_id=1, source_target_pairs={{1,0},{2,1},{3,2},{4,3},{5,4},{6,5},{7,6},{9,8},{10,9},{11,10},{12... | collective-permute-start | bytes 3145736 | tf_op jit(solution)/shard_map/ppermute | solution.py:140
  180.6 71.7 %collective-permute-start.2 = (bf16[1,16,256,128]{3,2,1,0:T(8,128)(2,1)}, bf16[1,16,256,128]{3,2,1,0:T(8,128)(2,1)}, u32[]{:S(2)}, u32[]{:S(2)}) collective-permute-start(bf16[1,16,256,128]{3,2,1,0:T(8,128)(2,1)} %get-tuple-element.12), channel_id=1, source_target_pairs={{0,1},{1,2},{2,3},{3,4},{4,5},{5,6},{6,7},{8,9},{9,10},{10,11},{11... | collective-permute-start | bytes 3145736 | tf_op jit(solution)/shard_map/ppermute | solution.py:139
Sparse Core Ops, SparseCore 0:
  9.8 55.2 all-gather.2
  105.5 70.6 all-gather.4
  178.6 66.6 all-reduce.1

commit v2 on v1

v2 whole, which is shorter than its diff:
```python
import functools
import math

import jax
import jax.numpy as jnp
from jax import lax
from jax.experimental import pallas as pl
from jax.experimental.pallas import tpu as pltpu
from jax.sharding import PartitionSpec as P

F32 = jnp.float32
BF16 = jnp.bfloat16
VMEM_LIMIT = 60 * 1024 * 1024


def shifted(rows, amount):
    size_z = rows.shape[1]
    lane = lax.broadcasted_iota(jnp.int32, rows.shape, 1)
    edge = 0 if amount == 1 else size_z - 1
    return jnp.where(lane == edge, 0.0, pltpu.roll(rows, amount % size_z, 1))


class Gather:
    def __init__(self, source, planes, local_sem, send_sem, recv_sem, halo_send, halo_recv, peers):
        self.source, self.planes = source, planes
        self.local_sem, self.send_sem, self.recv_sem = local_sem, send_sem, recv_sem
        self.halo_send, self.halo_recv = halo_send, halo_recv
        self.size_x, self.size_y, self.part, self.size_z = source.shape
        self.peers = peers
        self.me = lax.axis_index("chan")
        self.slab = lax.axis_index("space")
        self.slabs = lax.axis_size("space")
        self.chans = self.part * peers
        self.has_lo, self.has_hi = self.slab > 0, self.slab < self.slabs - 1
        self.order = [1] + ([self.size_x] if self.size_x > 1 else []) + list(range(2, self.size_x))
        me = self.me
        if peers == 4:
            across = me // 2 * 2 + (1 - me % 2)
            along = (1 - me // 2) * 2 + me % 2
            self.owners = [me, across, along, 3 - me]
            self.near = [1, 2]
        else:
            self.owners = [(me + r) % peers for r in range(peers)]
            self.near = list(range(1, peers))

    def block(self, q, owner):
        rows = pl.ds(pl.multiple_of(q * self.chans + owner * self.part, self.part), self.part)
        return self.planes.at[rows, self.size_z : (self.size_y + 1) * self.size_z]

    def back(self, slot):
        return slot if self.peers == 4 else self.peers - slot

    def chan_copy(self, q, slot_held, toward, slot_there):
        return pltpu.make_async_remote_copy(
            src_ref=self.block(q, self.owners[slot_held]),
            dst_ref=self.block(q, self.owners[slot_held]),
            send_sem=self.send_sem.at[q, slot_there],
            recv_sem=self.recv_sem.at[q, slot_there],
            device_id=(self.me, self.slab) if toward is None else (self.owners[toward], self.slab),
            device_id_type=pl.DeviceIdType.MESH,
        )

    def arrived(self, q, slot):
        pltpu.make_async_remote_copy(
            src_ref=self.block(q, self.owners[slot]),
            dst_ref=self.block(q, self.owners[slot]),
            send_sem=self.send_sem.at[q, slot],
            recv_sem=self.recv_sem.at[q, slot],
            device_id=(self.owners[1], self.slab),
            device_id_type=pl.DeviceIdType.MESH,
        ).wait_recv()

    def halo_copy(self, slot, up):
        mine, theirs = (self.size_x, 0) if up else (1, self.size_x + 1)
        return pltpu.make_async_remote_copy(
            src_ref=self.block(mine, self.owners[slot]),
            dst_ref=self.block(theirs, self.owners[slot]),
            send_sem=self.halo_send.at[int(up), slot],
            recv_sem=self.halo_recv.at[int(up), slot],
            device_id=(self.me, self.slab + 1 if up else self.slab - 1),
            device_id_type=pl.DeviceIdType.MESH,
        )

    def halo_pass(self, q, slot):
        if q == self.size_x:

            @pl.when(self.has_hi)
            def _():
                self.halo_copy(slot, True).start()

        if q == 1:

            @pl.when(self.has_lo)
            def _():
                self.halo_copy(slot, False).start()

    def local_copy(self, q, y):
        rows = pl.ds(pl.multiple_of(q * self.chans + self.me * self.part, self.part), self.part)
        lanes = pl.ds(pl.multiple_of((y + 1) * self.size_z, self.size_z), self.size_z)
        return pltpu.make_async_copy(
            self.source.at[q - 1, y], self.planes.at[rows, lanes], self.local_sem.at[q]
        )

    def begin(self):
        for q in self.order:

            def put(y, _, q=q):
                self.local_copy(q, y).start()
                return 0

            lax.fori_loop(0, self.size_y, put, 0)
        barrier = pltpu.get_barrier_semaphore()
        for slot in range(1, self.peers):
            pl.semaphore_signal(
                barrier, inc=1, device_id=(self.owners[slot], self.slab), device_id_type=pl.DeviceIdType.MESH
            )
        for step in (1, self.slabs - 1):
            beside = (self.slab + step) % self.slabs
            pl.semaphore_signal(
                barrier, inc=1, device_id=(self.me, beside), device_id_type=pl.DeviceIdType.MESH
            )

        edge = jnp.zeros((self.planes.shape[0], self.size_z), BF16)
        self.planes[:, 0 : self.size_z] = edge
        self.planes[:, (self.size_y + 1) * self.size_z : (self.size_y + 2) * self.size_z] = edge
        cells = slice(self.size_z, (self.size_y + 1) * self.size_z)
        blank = jnp.zeros((self.chans, self.size_y * self.size_z), BF16)

        @pl.when(jnp.logical_not(self.has_lo))
        def _():
            self.planes[0 : self.chans, cells] = blank

        @pl.when(jnp.logical_not(self.has_hi))
        def _():
            self.planes[(self.size_x + 1) * self.chans : (self.size_x + 2) * self.chans, cells] = blank

        pl.semaphore_wait(barrier, self.peers + 1)

        for q in self.order:

            def done(y, _, q=q):
                self.local_copy(q, y).wait()
                return 0

            lax.fori_loop(0, self.size_y, done, 0)
            for slot in self.near:
                self.chan_copy(q, 0, slot, self.back(slot)).start()
            self.halo_pass(q, 0)

    def relay(self, stage, q, slot):
        return self.peers == 4 and slot == (1 if stage % 2 else 2)

    def take_near(self, stage):
        q = self.order[stage]
        for slot in self.near:
            self.arrived(q, slot)
            if self.relay(stage, q, slot):
                self.chan_copy(q, slot, 3 - slot, 3).start()
            self.halo_pass(q, slot)

    def take_far(self, stage):
        q = self.order[stage]
        if self.peers == 4:
            self.arrived(q, 3)
            self.halo_pass(q, 3)

    def take_halo(self, up):
        @pl.when(self.has_lo if up else self.has_hi)
        def _():
            for slot in range(self.peers):
                mine, theirs = (self.size_x, 0) if up else (1, self.size_x + 1)
                pltpu.make_async_remote_copy(
                    src_ref=self.block(mine, self.owners[slot]),
                    dst_ref=self.block(theirs, self.owners[slot]),
                    send_sem=self.halo_send.at[int(up), slot],
                    recv_sem=self.halo_recv.at[int(up), slot],
                    device_id=(self.me, self.slab - 1 if up else self.slab + 1),
                    device_id_type=pl.DeviceIdType.MESH,
                ).wait_recv()

    def finish(self):
        for stage, q in enumerate(self.order):
            for slot in self.near:
                self.chan_copy(q, 0, slot, self.back(slot)).wait_send()
                if self.relay(stage, q, slot):
                    self.chan_copy(q, slot, 3 - slot, 3).wait_send()
        for up, there in ((True, self.has_hi), (False, self.has_lo)):

            @pl.when(there)
            def _(up=up):
                for slot in range(self.peers):
                    self.halo_copy(slot, up).wait_send()


def add_plane(planes, w_ref, acc, q, started, chans, size_y, size_z):
    size_x, rows, _ = acc.shape
    taps = [dx for dx in range(3) if 0 <= q - dx < size_x]
    first, last = taps[0], taps[-1] + 1
    count = 2

    def step(index, _):
        y = index * count
        total = None
        for dy in range(3):
            lanes = pl.ds(pl.multiple_of((y + dy) * size_z, size_z), count * size_z)
            part = jnp.dot(
                w_ref[dy, first * rows : last * rows],
                planes[q * chans : (q + 1) * chans, lanes],
                preferred_element_type=F32,
            )
            total = part if total is None else total + part
        lanes = pl.ds(pl.multiple_of(y * size_z, size_z), count * size_z)
        for dx in taps:
            part = total[(dx - first) * rows : (dx - first + 1) * rows]
            if q - dx in started:
                acc[q - dx, :, lanes] += part
            else:
                acc[q - dx, :, lanes] = part
        return 0

    lax.fori_loop(0, size_y // count, step, 0)
    started.update(q - dx for dx in taps)


def tap_sum(acc, x, outs, lanes):
    return (
        acc[x, outs : 2 * outs, lanes]
        + shifted(acc[x, 0:outs, lanes], 1)
        + shifted(acc[x, 2 * outs : 3 * outs, lanes], -1)
    )


def conv(gather, w_ref, acc, finish_plane, aside):
    size_x, chans, size_y, size_z = gather.size_x, gather.chans, gather.size_y, gather.size_z
    started, count, left = set(), {x: 3 for x in range(size_x)}, list(aside)

    def plane(q):
        add_plane(gather.planes, w_ref, acc, q, started, chans, size_y, size_z)
        for dx in range(3):
            if q - dx in count:
                count[q - dx] -= 1
                if count[q - dx] == 0:
                    finish_plane(q - dx)

    gather.begin()
    stages = len(gather.order)
    for stage in range(stages):
        if left:
            left.pop(0)()
        gather.take_near(stage)
        if stage:
            gather.take_far(stage - 1)
            plane(gather.order[stage - 1])
    gather.take_halo(True)
    plane(0)
    gather.take_halo(False)
    plane(size_x + 1)
    gather.take_far(stages - 1)
    plane(gather.order[-1])
    gather.finish()


def forward_kernel(peers, vol_ref, w_ref, bias_ref, cot_ref, out_ref, grad_ref, sum_ref, planes, acc, three, *sems):
    gather = Gather(vol_ref, planes, *sems, peers)
    size_x, size_y, outs, size_z = cot_ref.shape

    def finish_plane(x):
        def step(y, _):
            lanes = pl.ds(pl.multiple_of(y * size_z, size_z), size_z)
            pre = tap_sum(acc, x, outs, lanes) + bias_ref[...]
            sig = jax.nn.sigmoid(pre)
            out_ref[x, y] = (pre * sig).astype(BF16)
            grad = cot_ref[x, y].astype(F32) * sig * (1.0 + pre * (1.0 - sig))
            held = grad.astype(BF16)
            grad_ref[x, y] = held
            grad = held.astype(F32)
            three[x, 0:outs, lanes] = shifted(grad, -1).astype(BF16)
            three[x, outs : 2 * outs, lanes] = held
            three[x, 2 * outs : 3 * outs, lanes] = shifted(grad, 1).astype(BF16)
            return 0

        lax.fori_loop(0, size_y, step, 0)

    conv(gather, w_ref, acc, finish_plane, ())
    sum_ref[...] = jnp.zeros_like(sum_ref)
    chans, cells = gather.chans, size_y * size_z

    def step(x, _):
        for dy in range(3):
            cube = planes[pl.ds(pl.multiple_of(x * chans, chans), 3 * chans), dy * size_z : dy * size_z + cells]
            sum_ref[dy] += lax.dot_general(
                three[x], cube, (((1,), (1,)), ((), ())), preferred_element_type=F32
            )
        return 0

    lax.fori_loop(0, size_x, step, 0)


def input_kernel(peers, grad_ref, w_ref, out_ref, planes, acc, *sems):
    gather = Gather(grad_ref, planes, *sems, peers)
    size_x, size_y, outs, size_z = out_ref.shape

    def finish_plane(x):
        def step(y, _):
            lanes = pl.ds(pl.multiple_of(y * size_z, size_z), size_z)
            out_ref[x, y] = tap_sum(acc, x, outs, lanes).astype(BF16)
            return 0

        lax.fori_loop(0, size_y, step, 0)

    conv(gather, w_ref, acc, finish_plane, ())


def call(kernel, args, outs, extra, rows, flops, identity):
    whole = pl.BlockSpec(memory_space=pltpu.VMEM)
    peers = lax.axis_size("chan")
    size_x, size_y, part, size_z = args[0].shape
    planes = size_x + 2
    size = sum(a.size * a.dtype.itemsize for a in args)
    return pl.pallas_call(
        functools.partial(kernel, peers),
        out_shape=outs,
        in_specs=[pl.BlockSpec(memory_space=pl.ANY)] + [whole] * (len(args) - 1),
        out_specs=jax.tree.map(lambda _: whole, outs),
        scratch_shapes=[
            pltpu.VMEM((planes * part * peers, (size_y + 2) * size_z), BF16),
            pltpu.VMEM((size_x, rows, size_y * size_z), F32),
            *extra,
            pltpu.SemaphoreType.DMA((planes,)),
            pltpu.SemaphoreType.DMA((planes, peers)),
            pltpu.SemaphoreType.DMA((planes, peers)),
            pltpu.SemaphoreType.DMA((2, peers)),
            pltpu.SemaphoreType.DMA((2, peers)),
        ],
        compiler_params=pltpu.CompilerParams(
            vmem_limit_bytes=VMEM_LIMIT, collective_id=identity, has_side_effects=True
        ),
        cost_estimate=pl.CostEstimate(flops=flops, bytes_accessed=size, transcendentals=0),
    )(*args)


def on_device(volume, kernel, bias, cotangent):
    size_x, size_y, chans_local, size_z = volume.shape
    taps, outs, chans = kernel.shape
    shape = jax.ShapeDtypeStruct
    flops = 2 * size_x * size_y * size_z * taps * outs * chans
    cube = kernel.reshape(3, 3, 3, outs, chans)
    w_forward = cube.transpose(1, 0, 2, 3, 4).reshape(3, 9 * outs, chans)
    turned = lax.all_to_all(kernel, "chan", split_axis=2, concat_axis=1, tiled=True)
    all_outs, ins = turned.shape[1], turned.shape[2]
    turned = turned.reshape(3, 3, 3, all_outs, ins)[::-1, ::-1, ::-1]
    w_input = turned.transpose(1, 0, 2, 4, 3).reshape(3, 9 * ins, all_outs)
    column = jnp.broadcast_to(bias.reshape(outs, 1), (outs, size_z))

    output, grad_pre, partial = call(
        forward_kernel,
        (volume, w_forward, column, cotangent),
        (
            shape(cotangent.shape, BF16),
            shape(cotangent.shape, BF16),
            shape((3, 3 * outs, 3 * chans), F32),
        ),
        [pltpu.VMEM((size_x, 3 * outs, size_y * size_z), BF16)],
        3 * outs,
        2 * flops,
        0,
    )
    summed = lax.psum(partial, "space") / math.sqrt(size_x * size_y * size_z * lax.axis_size("space"))
    weight_grad = summed.reshape(3, 3, outs, 3, chans).transpose(3, 0, 1, 2, 4).reshape(taps, outs, chans)
    input_grad = call(input_kernel, (grad_pre, w_input), shape(volume.shape, BF16), [], 3 * ins, flops, 1)
    return output, input_grad, weight_grad


def solution(mesh):
    return jax.shard_map(
        on_device,
        mesh=mesh,
        in_specs=(
            P("space", None, "chan", None),
            P(None, "chan", None),
            P("chan"),
            P("space", None, "chan", None),
        ),
        out_specs=(
            P("space", None, "chan", None),
            P("space", None, "chan", None),
            P(None, "chan", None),
        ),
        check_vma=False,
    )
```

time: 281 us -> 192 us (0.68)
  waiting for transfers between devices: 152 us -> 0.04 us
  Pallas kernels: 68.1 us -> 145 us
  starting transfers between devices: 14.2 us -> 5.33 us
  local copies, waits for them, and re-layouts: 29.6 us -> 24.8 us
    all_gather x2 -> x0, waiting for transfers between devices: 101 us -> none  [the longest x1 57.2 us: on_device(): gathered = lax.all_gather(volume, 'chan', axis=2, tiled=True)]
    pallas_call x3 -> x2, Pallas kernels: 68.1 us -> 145 us  [call(): pl.pallas_call(functools.partial(kernel, peers), out_shape=outs, in_specs...]
    psum x1, waiting for transfers between devices: 50.1 us -> 0.02 us  [on_device(): lax.psum(partial, 'space')]
    ppermute x4 -> x0, starting transfers between devices: 10.6 us -> none  [the longest x2 8.05 us: with_neighbours(): lo = lax.ppermute(cells[-1:], 'space', up)]
    slice x2 -> x0, local copies, waits for them, and re-layouts: 5.81 us -> none  [with_neighbours(): hi = lax.ppermute(cells[:1], 'space', down)]
    unnamed x7 -> x13, local copies, waits for them, and re-layouts: 7.28 us -> 12.2 us
    reshape x2 -> x0, local copies, waits for them, and re-layouts: 4.24 us -> none  [the longest x1 2.13 us: on_device(): w_input = turned.transpose(1, 2, 4, 0, 3).reshape(3, 3 * ins, 3 * all_outs)]
  transfers between devices with their start and end apart: 8 -> 2, of which waited for: 3 -> 0; matrix products, arithmetic and copies ran while one was open for 10% -> 6% of each run, Pallas kernels for 6% -> 75%
where the time goes in v2:
time: 192 us
  Pallas kernels  145 us (76%)
  local copies, waits for them, and re-layouts  24.8 us (13%)
  between operations  14.1 us (7%)
  starting transfers between devices  5.33 us (3%)
  other arithmetic  2.82 us (1%)
    pallas_call x2, Pallas kernels, call(): pl.pallas_call(functools.partial(kernel, peers), out_shape=outs, in_specs...  145 us
    unnamed x13, local copies, waits for them, and re-layouts  12.2 us
    all_to_all x1, starting transfers between devices, on_device(): lax.all_to_all(kernel, 'chan', split_axis=2, concat_axis=1, tiled=True)  5.32 us
  transfers between devices with their start and end apart: 2, of which 0 were waited for; matrix products, arithmetic and copies ran while one was open for 6% of the time, Pallas kernels for 75%

profile of v2, /device:TPU:0, one launch (start us, length us, event | category | flops | bytes accessed | tf_op | source)
XLA Modules:
  0.0 191.7 jit_solution(2293078169407697221)
XLA Ops:
  7.2 3.9 %copy.17 = bf16[27,64,256]{1,0,2:T(8,128)(2,1)S(1)} copy(bf16[27,64,256]{2,1,0:T(8,128)(2,1)} %param.5) | data formatting | bytes 1769472 | tf_op args[1]
  11.1 0.0 copy-start
  11.1 2.4 %reshape.33 = bf16[4,2,55296]{2,1,0:T(2,128)(2,1)} reshape(bf16[256,27,64]{2,1,0:T(8,128)(2,1)S(1)} %bitcast.19) | data formatting | bytes 1769472
  13.5 0.0 copy-start.3
  13.5 5.3 %all-to-all-start = ((bf16[4,2,55296]{2,1,0:T(2,128)(2,1)}), bf16[4,2,55296]{2,1,0:T(2,128)(2,1)}, u32[]{:S(2)}, u32[]{:S(2)}) async-start(bf16[4,2,55296]{2,1,0:T(2,128)(2,1)} %reshape.33), calls=%async_computation | async-start | bytes 1769472 | tf_op jit(solution)/shard_map/all_to_all | solution.py:349
  18.8 0.0 all-reduce.2.cloned.1.call-start
  18.8 0.0 copy-done
  18.8 1.0 copy.16
  19.8 0.0 copy-done.3
  19.8 0.7 broadcast_in_dim.2.bias_ref
  20.5 83.3 %shard_map.67 = (bf16[4,16,64,128]{3,2,1,0:T(8,128)(2,1)}, bf16[4,16,64,128]{3,2,1,0:T(8,128)(2,1)}, f32[3,192,768]{2,1,0:T(8,128)}) custom-call(bf16[4,16,64,128]{3,2,1,0:T(8,128)(2,1)} %vol_ref.1, bf16[3,576,256]{2,1,0:T(8,128)(2,1)} %bitcast.23, f32[64,128]{1,0:T(8,128)} %broadcast_in_dim.2.bias_ref, bf16[4,16,64,128]{3,2,1,0:T(8,128)(2,1)} %cot_ref.1), custom_call_target="tpu_custom_call" | custom-call | flops 14495514624 | bytes 3014656 | tf_op jit(solution)/shard_map/pallas_call | solution.py:320
  103.8 0.0 all-reduce.2.cloned.1.call-update
  103.8 0.0 all-to-all-done
  103.8 3.3 %reshape.34 = bf16[256,27,64]{2,1,0:T(8,128)(2,1)S(1)} reshape(bf16[4,2,55296]{2,1,0:T(2,128)(2,1)} %all-to-all-done) | data formatting | bytes 1769472
  107.1 2.6 %copy.22 = bf16[27,64,4,64]{1,2,3,0:T(4,128)(2,1)} copy(bf16[27,64,4,64]{1,0,3,2:T(8,128)(2,1)S(1)} %bitcast.18) | data formatting | bytes 1769472 | tf_op jit(solution)/shard_map/all_to_all | solution.py:349
  109.7 3.1 %reshape.29 = bf16[3,3,3,256,64]{3,4,2,1,0:T(8,128)(2,1)S(1)} reshape(bf16[27,4,64,64]{2,1,3,0:T(4,128)(2,1)} %bitcast.20) | data formatting | bytes 1769472 | tf_op jit(solution)/shard_map/reshape | solution.py:351
  112.8 0.1 reverse_bitcast_fusion
  112.9 1.0 copy.19
  113.9 61.3 %shard_map.68 = bf16[4,16,64,128]{3,2,1,0:T(8,128)(2,1)} custom-call(bf16[4,16,64,128]{3,2,1,0:T(8,128)(2,1)} %get-tuple-element.7.grad_ref, bf16[3,576,256]{2,1,0:T(8,128)(2,1)} %bitcast.24), custom_call_target="tpu_custom_call" | custom-call | flops 7247757312 | bytes 1933312 | tf_op jit(solution)/shard_map/pallas_call | solution.py:320
  175.2 0.0 all-reduce.2.cloned.1.call-done
  175.2 2.8 %broadcast_multiply_fusion = f32[3,192,768]{2,1,0:T(8,128)} fusion(f32[3,192,768]{2,1,0:T(8,128)} %all-reduce.2.cloned.1.call-done), kind=kLoop, calls=%fused_computation.1 | loop fusion | flops 442368 | bytes 3538944 | tf_op jit(solution)/shard_map/div | solution.py:368
  178.0 2.7 %reshape.31 = f32[3,3,64,3,256]{4,3,2,1,0:T(4,128)S(1)} reshape(f32[3,192,768]{2,1,0:T(8,128)} %broadcast_multiply_fusion) | data formatting | bytes 3538944 | tf_op jit(solution)/shard_map/reshape | solution.py:369
  180.8 0.0 copy-start.1
  180.8 1.5 copy.20
  182.3 0.0 copy-start.2
  182.3 0.0 copy-done.1
  182.3 1.0 copy.26
  183.3 0.6 copy-done.2
  183.9 1.0 copy.27
Async XLA Ops:
  11.1 7.7 %copy-start = (bf16[27,64,256]{2,1,0:T(8,128)(2,1)S(1)}, bf16[27,64,256]{2,1,0:T(8,128)(2,1)}, u32[]{:S(2)}) copy-start(bf16[27,64,256]{2,1,0:T(8,128)(2,1)} %param.5) | copy-start | bytes 2654212
  13.5 6.3 %copy-start.3 = (f32[64]{0:T(128)S(1)}, f32[64]{0:T(128)}, u32[]{:S(2)}) copy-start(f32[64]{0:T(128)} %param.6) | copy-start | bytes 772
  13.5 90.3 %all-to-all-start = ((bf16[4,2,55296]{2,1,0:T(2,128)(2,1)}), bf16[4,2,55296]{2,1,0:T(2,128)(2,1)}, u32[]{:S(2)}, u32[]{:S(2)}) async-start(bf16[4,2,55296]{2,1,0:T(2,128)(2,1)} %reshape.33), calls=%async_computation | async-start | bytes 1769472 | tf_op jit(solution)/shard_map/all_to_all | solution.py:349
  18.8 156.4 %all-reduce.2.cloned.1.call-start = ((), (), s32[]{:S(2)}) async-start(), calls=%async_computation.1 | async-start | bytes 3538944 | tf_op jit(solution)/shard_map/psum | solution.py:368
  180.8 1.5 copy-start.1
  182.3 1.6 copy-start.2
Sparse Core Ops, SparseCore 0:
  103.9 68.7 all-reduce.1

commit v3 on v2

--- a/solution.py
+++ b/solution.py
@@ -143,9 +143,14 @@
                 return 0
 
             lax.fori_loop(0, self.size_y, done, 0)
-            for slot in self.near:
-                self.chan_copy(q, 0, slot, self.back(slot)).start()
-            self.halo_pass(q, 0)
+        for stage in range(min(2, len(self.order))):
+            self.send_own(stage)
+
+    def send_own(self, stage):
+        q = self.order[stage]
+        for slot in self.near:
+            self.chan_copy(q, 0, slot, self.back(slot)).start()
+        self.halo_pass(q, 0)
 
     def relay(self, stage, q, slot):
         return self.peers == 4 and slot == (1 if stage % 2 else 2)
@@ -157,6 +162,8 @@
             if self.relay(stage, q, slot):
                 self.chan_copy(q, slot, 3 - slot, 3).start()
             self.halo_pass(q, slot)
+        if stage + 2 < len(self.order):
+            self.send_own(stage + 2)
 
     def take_far(self, stage):
         q = self.order[stage]
@@ -204,7 +211,7 @@
         for dy in range(3):
             lanes = pl.ds(pl.multiple_of((y + dy) * size_z, size_z), count * size_z)
             part = jnp.dot(
-                w_ref[dy, first * rows : last * rows],
+                w_ref[first:last, dy].reshape((last - first) * rows, chans),
                 planes[q * chans : (q + 1) * chans, lanes],
                 preferred_element_type=F32,
             )
@@ -288,17 +295,30 @@
     def step(x, _):
         for dy in range(3):
             cube = planes[pl.ds(pl.multiple_of(x * chans, chans), 3 * chans), dy * size_z : dy * size_z + cells]
-            sum_ref[dy] += lax.dot_general(
+            part = lax.dot_general(
                 three[x], cube, (((1,), (1,)), ((), ())), preferred_element_type=F32
             )
+            for dx in range(3):
+                sum_ref[dx, dy] += part[:, dx * chans : (dx + 1) * chans]
         return 0
 
     lax.fori_loop(0, size_x, step, 0)
-
-
-def input_kernel(peers, grad_ref, w_ref, out_ref, planes, acc, *sems):
+    sum_ref[...] = sum_ref[...] * (1.0 / math.sqrt(size_x * cells * gather.slabs))
+
+
+def input_kernel(peers, grad_ref, pieces_ref, out_ref, planes, acc, w_ref, *sems):
     gather = Gather(grad_ref, planes, *sems, peers)
     size_x, size_y, outs, size_z = out_ref.shape
+
+    def turn():
+        def step(tap, _):
+            dx, dy, dz = tap // 9, tap // 3 % 3, tap % 3
+            whole = jnp.concatenate([pieces_ref[i, 26 - tap] for i in range(peers)], axis=0)
+            rows = pl.ds(pl.multiple_of(dz * outs, outs), outs)
+            w_ref[dx, dy, rows] = whole.astype(F32).T.astype(BF16)
+            return 0
+
+        lax.fori_loop(0, 27, step, 0)
 
     def finish_plane(x):
         def step(y, _):
@@ -308,7 +328,7 @@
 
         lax.fori_loop(0, size_y, step, 0)
 
-    conv(gather, w_ref, acc, finish_plane, ())
+    conv(gather, w_ref, acc, finish_plane, (turn,))
 
 
 def call(kernel, args, outs, extra, rows, flops, identity):
@@ -344,12 +364,11 @@
     taps, outs, chans = kernel.shape
     shape = jax.ShapeDtypeStruct
     flops = 2 * size_x * size_y * size_z * taps * outs * chans
-    cube = kernel.reshape(3, 3, 3, outs, chans)
-    w_forward = cube.transpose(1, 0, 2, 3, 4).reshape(3, 9 * outs, chans)
-    turned = lax.all_to_all(kernel, "chan", split_axis=2, concat_axis=1, tiled=True)
-    all_outs, ins = turned.shape[1], turned.shape[2]
-    turned = turned.reshape(3, 3, 3, all_outs, ins)[::-1, ::-1, ::-1]
-    w_input = turned.transpose(1, 0, 2, 4, 3).reshape(3, 9 * ins, all_outs)
+    w_forward = kernel.reshape(3, 3, 3 * outs, chans)
+    peers = lax.axis_size("chan")
+    ins, all_outs = chans // peers, outs * peers
+    pieces = kernel.reshape(taps, outs, peers, ins).transpose(2, 0, 1, 3)
+    pieces = lax.all_to_all(pieces, "chan", split_axis=0, concat_axis=0, tiled=True)
     column = jnp.broadcast_to(bias.reshape(outs, 1), (outs, size_z))
 
     output, grad_pre, partial = call(
@@ -358,16 +377,23 @@
         (
             shape(cotangent.shape, BF16),
             shape(cotangent.shape, BF16),
-            shape((3, 3 * outs, 3 * chans), F32),
+            shape((3, 3, 3 * outs, chans), F32),
         ),
         [pltpu.VMEM((size_x, 3 * outs, size_y * size_z), BF16)],
         3 * outs,
         2 * flops,
         0,
     )
-    summed = lax.psum(partial, "space") / math.sqrt(size_x * size_y * size_z * lax.axis_size("space"))
-    weight_grad = summed.reshape(3, 3, outs, 3, chans).transpose(3, 0, 1, 2, 4).reshape(taps, outs, chans)
-    input_grad = call(input_kernel, (grad_pre, w_input), shape(volume.shape, BF16), [], 3 * ins, flops, 1)
+    weight_grad = lax.psum(partial, "space").reshape(taps, outs, chans)
+    input_grad = call(
+        input_kernel,
+        (grad_pre, pieces),
+        shape(volume.shape, BF16),
+        [pltpu.VMEM((3, 3, 3 * ins, all_outs), BF16)],
+        3 * ins,
+        flops,
+        1,
+    )
     return output, input_grad, weight_grad
 
 

time: 192 us -> 178 us (0.927)
  local copies, waits for them, and re-layouts: 24.8 us -> 12.3 us
  waiting for transfers between devices: 0.04 us -> 7.23 us
  Pallas kernels: 145 us -> 139 us
  other arithmetic: 2.82 us -> 0 us
    psum x1, waiting for transfers between devices: 0.02 us -> 7.21 us  [on_device(): weight_grad = lax.psum(partial, 'space').reshape(taps, outs, chans)]
    pallas_call x2, Pallas kernels: 145 us -> 139 us  [call(): pl.pallas_call(functools.partial(kernel, peers), out_shape=outs, in_specs...]
    unnamed x13, local copies, waits for them, and re-layouts: 12.2 us -> 8.18 us
    reshape x3 -> x2, local copies, waits for them, and re-layouts: 6.79 us -> 3.41 us  [on_device(): pieces = kernel.reshape(taps, outs, peers, ins).transpose(2, 0, 1, 3)]
    div x1 -> x0, other arithmetic: 2.82 us -> none  [on_device(): lax.psum(partial, 'space')]
    all_to_all x1 -> x0, local copies, waits for them, and re-layouts: 2.61 us -> none  [on_device(): lax.all_to_all(kernel, 'chan', split_axis=2, concat_axis=1, tiled=True)]
    transpose x3 -> x0, local copies, waits for them, and re-layouts: 2.59 us -> none  [the longest x1 1.53 us: on_device(): summed.reshape(3, 3, outs, 3, chans).transpose(3, 0, 1, 2, 4)]
  transfers between devices with their start and end apart: 2 -> 2, of which waited for: 0 -> 1; matrix products, arithmetic and copies ran while one was open for 6% -> 2% of each run, Pallas kernels for 75% -> 78%
where the time goes in v3:
time: 178 us; the launch traced here: 177 us
  Pallas kernels  139 us (78%)
  between operations  14.1 us (8%)
  local copies, waits for them, and re-layouts  12.3 us (7%)
  waiting for transfers between devices  7.23 us (4%)
  starting transfers between devices  5.19 us (3%)
    pallas_call x2, Pallas kernels, call(): pl.pallas_call(functools.partial(kernel, peers), out_shape=outs, in_specs...  139 us
    unnamed x13, local copies, waits for them, and re-layouts  8.18 us
    psum x1, waiting for transfers between devices, on_device(): weight_grad = lax.psum(partial, 'space').reshape(taps, outs, chans)  7.21 us
    all_to_all x1, starting transfers between devices, on_device(): lax.all_to_all(pieces, 'chan', split_axis=0, concat_axis=0, tiled=True)  5.19 us
  transfers between devices with their start and end apart: 2, of which 1 were waited for; matrix products, arithmetic and copies ran while one was open for 2% of the time, Pallas kernels for 78%

profile of v3, /device:TPU:0, one launch (start us, length us, event | category | flops | bytes accessed | tf_op | source)
XLA Modules:
  0.0 177.3 jit_solution(12326371878960706362)
XLA Ops:
  7.2 3.0 %reshape.18 = bf16[27,64,4,64]{3,2,1,0:T(4,128)(2,1)S(1)} reshape(bf16[27,64,256]{2,1,0:T(8,128)(2,1)} %param.5) | data formatting | bytes 1769472 | tf_op jit(solution)/shard_map/reshape | solution.py:370
  10.1 0.4 copy.9
  10.6 0.0 copy-start.3
  10.6 2.5 %reshape.20 = bf16[4,2,55296]{2,1,0:T(2,128)(2,1)} reshape(bf16[4,27,64,64]{3,2,1,0:T(8,128)(2,1)S(1)} %bitcast.5) | data formatting | bytes 1769472
  13.1 5.2 %all-to-all-start = ((bf16[4,2,55296]{2,1,0:T(2,128)(2,1)}), bf16[4,2,55296]{2,1,0:T(2,128)(2,1)S(1)}, u32[]{:S(2)}, u32[]{:S(2)}) async-start(bf16[4,2,55296]{2,1,0:T(2,128)(2,1)} %reshape.20), calls=%async_computation | async-start | bytes 1769472 | tf_op jit(solution)/shard_map/all_to_all | solution.py:371
  18.3 0.0 all-reduce.2.cloned.1.call-start
  18.3 0.0 copy-done.3
  18.3 0.7 broadcast_in_dim.2.bias_ref
  19.0 81.6 %shard_map.67 = (bf16[4,16,64,128]{3,2,1,0:T(8,128)(2,1)}, bf16[4,16,64,128]{3,2,1,0:T(8,128)(2,1)}, f32[3,3,192,256]{3,2,1,0:T(8,128)}) custom-call(bf16[4,16,64,128]{3,2,1,0:T(8,128)(2,1)} %vol_ref.1, bf16[3,3,192,256]{3,2,1,0:T(8,128)(2,1)} %bitcast.7, f32[64,128]{1,0:T(8,128)} %broadcast_in_dim.2.bias_ref, bf16[4,16,64,128]{3,2,1,0:T(8,128)(2,1)} %cot_ref.1), custom_call_target="tpu_custom_call" | custom-call | flops 14495514624 | bytes 3014656 | tf_op jit(solution)/shard_map/pallas_call | solution.py:340
  100.6 0.0 all-reduce.2.cloned.1.call-update
  100.6 0.0 all-to-all-done
  100.6 2.5 %reshape.21.pieces_ref = bf16[4,27,64,64]{3,2,1,0:T(8,128)(2,1)} reshape(bf16[4,2,55296]{2,1,0:T(2,128)(2,1)S(1)} %all-to-all-done) | data formatting | bytes 1769472
  103.1 0.0 copy-start.1
  103.2 56.9 %shard_map.68 = bf16[4,16,64,128]{3,2,1,0:T(8,128)(2,1)} custom-call(bf16[4,16,64,128]{3,2,1,0:T(8,128)(2,1)} %get-tuple-element.7.grad_ref, bf16[4,27,64,64]{3,2,1,0:T(8,128)(2,1)} %reshape.21.pieces_ref), custom_call_target="tpu_custom_call" | custom-call | flops 7247757312 | bytes 1933312 | tf_op jit(solution)/shard_map/pallas_call | solution.py:340
  160.1 0.0 copy-start.2
  160.1 7.2 %all-reduce.2.cloned.1.call-done = f32[27,64,256]{2,1,0:T(8,128)} async-done(((f32[27,64,256]{2,1,0:T(8,128)}), f32[27,64,256]{2,1,0:T(8,128)}) %all-reduce.2.cloned.1.call-update) | async-done | bytes 1769488 | tf_op jit(solution)/shard_map/psum | solution.py:387
  167.3 0.0 copy-done.1
  167.3 0.0 copy-start
  167.3 1.0 copy.14
  168.3 0.0 copy-done.2
  168.3 1.0 copy.15
  169.3 0.0 copy-done
  169.3 1.2 copy.16
Async XLA Ops:
  10.6 7.7 %copy-start.3 = (f32[64]{0:T(128)S(1)}, f32[64]{0:T(128)}, u32[]{:S(2)}) copy-start(f32[64]{0:T(128)} %param.6) | copy-start | bytes 772
  13.1 87.5 %all-to-all-start = ((bf16[4,2,55296]{2,1,0:T(2,128)(2,1)}), bf16[4,2,55296]{2,1,0:T(2,128)(2,1)S(1)}, u32[]{:S(2)}, u32[]{:S(2)}) async-start(bf16[4,2,55296]{2,1,0:T(2,128)(2,1)} %reshape.20), calls=%async_computation | async-start | bytes 1769472 | tf_op jit(solution)/shard_map/all_to_all | solution.py:371
  18.3 149.0 %all-reduce.2.cloned.1.call-start = ((), (), s32[]{:S(2)}) async-start(), calls=%async_computation.1 | async-start | bytes 3538944 | tf_op jit(solution)/shard_map/psum | solution.py:387
  103.1 64.2 %copy-start.1 = (bf16[4,16,64,128]{3,2,1,0:T(8,128)(2,1)S(1)}, bf16[4,16,64,128]{3,2,1,0:T(8,128)(2,1)}, u32[]{:S(2)}) copy-start(bf16[4,16,64,128]{3,2,1,0:T(8,128)(2,1)} %get-tuple-element.12) | copy-start | bytes 3145732
  160.1 8.2 %copy-start.2 = (bf16[4,16,64,128]{3,2,1,0:T(8,128)(2,1)S(1)}, bf16[4,16,64,128]{3,2,1,0:T(8,128)(2,1)}, u32[]{:S(2)}) copy-start(bf16[4,16,64,128]{3,2,1,0:T(8,128)(2,1)} %shard_map.68) | copy-start | bytes 3145732
  167.3 1.9 %copy-start = (f32[27,64,256]{2,1,0:T(8,128)S(1)}, f32[27,64,256]{2,1,0:T(8,128)}, u32[]{:S(2)}) copy-start(f32[27,64,256]{2,1,0:T(8,128)} %all-reduce.2.cloned.1.call-done) | copy-start | bytes 5308420
Sparse Core Ops, SparseCore 0:
  100.7 66.5 all-reduce.1
